TPU v7x, 32 devices: a whole 2x2x4 slice. The times are simulated.
32 devices in a mesh: shard: 16 (over z, y, x), rep: 2 (over core).
Axes of the slice: x: 2, y: 2, z: 4, core: 2. Of those that a mesh axis runs over, the one named last changes fastest.
Arguments:
- dense_feats: bfloat16 [4096, 13], P(('shard', 'rep')), may hold values from -6 to 6
- lookup_ids: int32 [4096, 13, 4], P(('shard', 'rep')), may hold values from 0 to 1023, as said below
- bag_lengths: int32 [4096, 13], P(('shard', 'rep')), may hold values from 1 to 4
- bottom_w1: bfloat16 [13, 512], replicated, may hold values from -1.75 to 1.75
- bottom_w2: bfloat16 [512, 256], replicated, may hold values from -0.25 to 0.25
- bottom_w3: bfloat16 [256, 128], replicated, may hold values from -0.375 to 0.375
- tables: bfloat16 [13, 1024, 128], P(None, 'shard'), may hold values from -3 to 3
- accum: float32 [13, 1024], P(None, 'shard'), may hold values from 0.05 to 1
- cross_down: bfloat16 [1792, 512], replicated, may hold values from -0.125 to 0.125
- cross_up: bfloat16 [512, 1792], replicated, may hold values from -0.25 to 0.25
- cross_bias: float32 [1792], replicated, may hold values from -3 to 3
- cotangent: bfloat16 [4096, 1792], P(('shard', 'rep')), may hold values from -0.3984375 to 0.3984375
Outputs:
- crossed: bfloat16 [4096, 1792], P(('shard', 'rep'))
- new_tables: float32 [13, 1024, 128], P(None, 'shard')
- new_accum: float32 [13, 1024], P(None, 'shard')
Inputs may be any that keep to these rules, and one draw needn't show every extreme that they name: `lookup_ids`: row r of a table is held by index r // 64 of shard. Among the 6656 slots of one device (used or not), at most 624 name rows held by any one index of shard, and in every draw one index of shard gets exactly 624 from every device. Only the first bag_lengths[s, t] slots of bag (s, t) are used.
All inputs are finite; a program needn't handle non-finite values.
Results may differ from a plain program's by a relative error of at most 0.0065.
Values may be sent and summed in bfloat16 or wider, within the bound.
A program may use at most 128 MiB of HBM per device.

v0:
```python
import jax
import jax.numpy as jnp
from jax import lax
from jax.sharding import PartitionSpec as P

step_size = 1.0
adagrad_eps = 1e-08
contract_first = (((0,), (0,)), ((), ()))
contract_last = (((1,), (1,)), ((), ()))


def per_device(
    dense_feats,
    lookup_ids,
    bag_lengths,
    bottom_w1,
    bottom_w2,
    bottom_w3,
    tables,
    accum,
    cross_down,
    cross_up,
    cross_bias,
    cotangent,
):
    shards = lax.axis_size("shard")
    batch_rows, table_count, pool_slots = lookup_ids.shape
    rows_dev = tables.shape[1]
    emb_width = tables.shape[2]
    slot_count = batch_rows * table_count * pool_slots
    mean_load = slot_count // shards
    capacity = mean_load + mean_load // 2
    send_width = shards * capacity
    local_count = table_count * rows_dev
    owners = lookup_ids // rows_dev
    local_rows = (
        lookup_ids
        - owners * rows_dev
        + (jnp.arange(table_count, dtype=jnp.int32) * rows_dev)[None, :, None]
    )
    live_mask = jnp.arange(pool_slots, dtype=jnp.int32)[None, None, :] < bag_lengths[:, :, None]
    owner_flat = owners.reshape(-1)
    block_size = 128
    block_total = slot_count // block_size
    owner_marks = (owner_flat[:, None] == jnp.arange(shards, dtype=jnp.int32)[None, :]).astype(
        jnp.bfloat16
    )
    owner_marks = owner_marks.reshape(block_total, block_size, shards)
    earlier = (jnp.arange(block_size)[:, None] > jnp.arange(block_size)[None, :]).astype(
        jnp.bfloat16
    )
    within = jnp.einsum("ij,bjn->bin", earlier, owner_marks, preferred_element_type=jnp.float32)
    totals = jnp.sum(owner_marks, axis=1, dtype=jnp.float32)
    lower_blocks = (jnp.arange(block_total)[:, None] > jnp.arange(block_total)[None, :]).astype(
        jnp.float32
    )
    before = jnp.dot(lower_blocks, totals, precision=lax.Precision.HIGHEST)
    positions = (
        jnp.sum((within + before[:, None, :]) * owner_marks, axis=2).reshape(-1).astype(jnp.int32)
    )
    slot_of = owner_flat * capacity + positions
    bag_count = batch_rows * table_count
    sample_block = min(64, batch_rows)
    block_rows = sample_block * table_count
    bag_blocks = bag_count // block_rows
    column_span = jnp.arange(send_width, dtype=jnp.int32)
    dest_blocks = slot_of.reshape(bag_blocks, block_rows, pool_slots)
    live_blocks = live_mask.reshape(bag_blocks, block_rows, pool_slots)

    def slot_marks(dest_part, live_part, slot):
        return (
            (dest_part[:, slot, None] == column_span[None, :]) & live_part[:, slot, None]
        ).astype(jnp.bfloat16)

    def bag_marks(dest_part, live_part):
        marks = slot_marks(dest_part, live_part, 0)
        for slot in range(1, pool_slots):
            marks = marks + slot_marks(dest_part, live_part, slot)
        return marks

    coded = jnp.where(live_mask, local_rows, -1).reshape(bag_blocks, block_rows, pool_slots) + 1
    digits = jnp.stack([coded % 128, coded // 128], axis=3).astype(jnp.float32).astype(jnp.bfloat16)

    def add_ids(carry, piece_list):
        dest_part, live_part, digit_part = piece_list
        for slot in range(pool_slots):
            carry = carry + lax.dot_general(
                slot_marks(dest_part, live_part, slot),
                digit_part[:, slot, :],
                contract_first,
                preferred_element_type=jnp.float32,
            )
        return (carry, None)

    digit_sum, _ = lax.scan(
        add_ids, jnp.zeros((send_width, 2), jnp.float32), (dest_blocks, live_blocks, digits)
    )
    send_ids = ((digit_sum[:, 0] + 128.0 * digit_sum[:, 1]).astype(jnp.int32) - 1).reshape(
        shards, capacity
    )
    table_rows_flat = tables.reshape(-1, emb_width)
    local_index = jnp.arange(local_count, dtype=jnp.int32)
    received = lax.all_to_all(send_ids, "shard", split_axis=0, concat_axis=0, tiled=True)
    row_flags = (received[..., None] == local_index).astype(jnp.bfloat16)
    picked = jnp.einsum(
        "ojk,kt->ojt", row_flags, table_rows_flat, preferred_element_type=jnp.float32
    ).astype(jnp.bfloat16)
    returned = lax.all_to_all(picked, "shard", split_axis=0, concat_axis=0, tiled=True)
    returned, owner_ids = (returned, received)
    returned_flat = returned.reshape(-1, emb_width)

    def pool_block(carry, piece_list):
        dest_part, live_part = piece_list
        return (
            carry,
            jnp.dot(
                bag_marks(dest_part, live_part), returned_flat, preferred_element_type=jnp.float32
            ),
        )

    _, pooled_blocks = lax.scan(pool_block, 0, (dest_blocks, live_blocks))
    pooled = pooled_blocks.reshape(batch_rows, table_count * emb_width)
    first_layer = jax.nn.relu(
        jnp.dot(dense_feats, bottom_w1, preferred_element_type=jnp.float32)
    ).astype(jnp.bfloat16)
    second_layer = jax.nn.relu(
        jnp.dot(first_layer, bottom_w2, preferred_element_type=jnp.float32)
    ).astype(jnp.bfloat16)
    third_layer = jax.nn.relu(
        jnp.dot(second_layer, bottom_w3, preferred_element_type=jnp.float32)
    ).astype(jnp.bfloat16)
    stacked = jnp.concatenate([third_layer, pooled.astype(jnp.bfloat16)], axis=1)
    low_rank = jnp.dot(stacked, cross_down, preferred_element_type=jnp.float32).astype(jnp.bfloat16)
    cross_hidden = jnp.dot(low_rank, cross_up, preferred_element_type=jnp.float32)
    widened = stacked.astype(jnp.float32)
    crossed = (widened * (cross_hidden + cross_bias) + widened).astype(jnp.bfloat16)
    cot_wide = cotangent.astype(jnp.float32)
    hidden_grad = (cot_wide * widened).astype(jnp.bfloat16)
    low_grad = lax.dot_general(
        hidden_grad, cross_up, contract_last, preferred_element_type=jnp.float32
    ).astype(jnp.bfloat16)
    back_term = lax.dot_general(
        low_grad, cross_down[emb_width:], contract_last, preferred_element_type=jnp.float32
    )
    pooled_grad = (
        cot_wide[:, emb_width:] * (cross_hidden[:, emb_width:] + cross_bias[emb_width:] + 1.0)
        + back_term
    ).astype(jnp.bfloat16)
    grad_blocks = pooled_grad.reshape(bag_blocks, block_rows, emb_width)

    def spread_block(carry, piece_list):
        dest_part, live_part, grad_part = piece_list
        return (
            carry
            + lax.dot_general(
                bag_marks(dest_part, live_part),
                grad_part,
                contract_first,
                preferred_element_type=jnp.float32,
            ),
            None,
        )

    spread, _ = lax.scan(
        spread_block,
        jnp.zeros((send_width, emb_width), jnp.float32),
        (dest_blocks, live_blocks, grad_blocks),
    )
    send_grads = spread.astype(jnp.bfloat16).reshape(shards, capacity, emb_width)
    received_rows = lax.all_to_all(send_grads, "shard", split_axis=0, concat_axis=0, tiled=True)
    target_flags = (owner_ids[..., None] == local_index).astype(jnp.bfloat16)
    group_grad = jnp.einsum(
        "jbp,jbm->pm", target_flags, received_rows, preferred_element_type=jnp.float32
    )
    accum_flat = accum.reshape(-1)
    row_share = lax.psum_scatter(
        group_grad.astype(jnp.bfloat16), "rep", scatter_dimension=0, tiled=True
    ).astype(jnp.float32)
    share_rows = row_share.shape[0]
    share_start = lax.axis_index("rep") * share_rows
    accum_share = lax.dynamic_slice_in_dim(accum_flat, share_start, share_rows, 0)
    table_share = lax.dynamic_slice_in_dim(table_rows_flat, share_start, share_rows, 0)
    share_accum = accum_share + jnp.mean(row_share * row_share, axis=1)
    share_tables = table_share.astype(jnp.float32) - step_size * row_share / (
        jnp.sqrt(share_accum)[:, None] + adagrad_eps
    )
    new_tables, new_accum = (
        lax.all_gather(share_tables.astype(jnp.bfloat16), "rep", axis=0, tiled=True).astype(
            share_tables.dtype
        ),
        lax.all_gather(share_accum.astype(jnp.bfloat16), "rep", axis=0, tiled=True).astype(
            share_accum.dtype
        ),
    )
    return (
        crossed,
        new_tables.reshape(table_count, rows_dev, emb_width),
        new_accum.reshape(table_count, rows_dev),
    )


def solution(mesh):
    in_specs = (
        P(("shard", "rep"), None),
        P(("shard", "rep"), None, None),
        P(("shard", "rep"), None),
        P(),
        P(),
        P(),
        P(None, "shard", None),
        P(None, "shard"),
        P(),
        P(),
        P(),
        P(("shard", "rep"), None),
    )
    out_specs = (P(("shard", "rep"), None), P(None, "shard", None), P(None, "shard"))
    return jax.shard_map(
        per_device, mesh=mesh, in_specs=in_specs, out_specs=out_specs, check_vma=False
    )
```

profile of v0, /device:TPU:0, one launch (start us, length us, event | category | flops | bytes accessed | tf_op | source)
XLA Modules:
  0.0 398.5 jit_solution(1305242695001960423)
XLA Ops:
  12.7 63.0 %while.37 = (s32[]{:T(128)}, f32[9984,2]{0,1:T(2,128)S(1)}, s32[2,832,4]{1,2,0:T(4,128)S(1)}, pred[2,832,4]{1,2,0:T(4,128)(4,1)S(1)}, bf16[2,832,4,2]{1,3,2,0:T(2,128)(2,1)S(1)}, /*index=5*/s32[]{:T(128)}, s32[]{:T(128)}) while((s32[]{:T(128)}, f32[9984,2]{0,1:T(2,128)S(1)}, s32[2,832,4]{1,2,0:T(4,128)S(1)}, ...), condition=%wide.region_3.4_spmd.clone.clone, body=%wide.region_2.3_spmd.clone.clone.sunk | while | flops 199460352 | bytes 767075 | solution.py:95
  13.2 7.2 %fusion.166 = f32[9984,2]{0,1:T(2,128)S(1)} fusion(s32[832]{0:T(1024)S(1)} %get-tuple-element.447, pred[832]{0:T(1024)(128)(4,1)S(1)} %get-tuple-element.448, bf16[832,4,2]{0,2,1:T(2,128)(2,1)S(1)} %dynamic-slice_bitcast_fusion.18), kind=kOutput, calls=%fused_computation.43.clone.1 | convolution fusion | flops 49840128 | bytes 88576 | tf_op jit(solution)/shard_map/while/body/eval_jaxpr/dot_general | solution.py:87
  20.3 7.2 %fusion.167 = f32[9984,2]{0,1:T(2,128)S(1)} fusion(s32[832]{0:T(1024)S(1)} %get-tuple-element.449, pred[832]{0:T(1024)(128)(4,1)S(1)} %get-tuple-element.450, bf16[832,4,2]{0,2,1:T(2,128)(2,1)S(1)} %dynamic-slice_bitcast_fusion.18), kind=kOutput, calls=%fused_computation.44.clone.1 | convolution fusion | flops 49840128 | bytes 88576 | tf_op jit(solution)/shard_map/while/body/eval_jaxpr/dot_general | solution.py:87
  27.5 7.2 %fusion.168 = f32[9984,2]{0,1:T(2,128)S(1)} fusion(s32[832]{0:T(1024)S(1)} %get-tuple-element.451, pred[832]{0:T(1024)(128)(4,1)S(1)} %get-tuple-element.452, bf16[832,4,2]{0,2,1:T(2,128)(2,1)S(1)} %dynamic-slice_bitcast_fusion.18), kind=kOutput, calls=%fused_computation.45.clone.1 | convolution fusion | flops 49840128 | bytes 88576 | tf_op jit(solution)/shard_map/while/body/eval_jaxpr/dot_general | solution.py:87
  34.7 7.2 %fusion.169 = f32[9984,2]{0,1:T(2,128)S(1)} fusion(f32[9984,2]{0,1:T(2,128)S(1)} %fusion.166, f32[9984,2]{0,1:T(2,128)S(1)} %fusion.167, f32[9984,2]{0,1:T(2,128)S(1)} %fusion.168, s32[832]{0:T(1024)S(1)} %get-tuple-element.453, pred[832]{0:T(1024)(128)(4,1)S(1)} %get-tuple-element.454, f32[9984,2]{0,1:T(2,128)S(1)} %get-tuple-element.476, ...), kind=kOutput, calls=%fused_computation.58.clone.1 | convolution fusion | flops 49939968 | bytes 408065 | tf_op jit(solution)/shard_map/while/body/eval_jaxpr/dot_general | solution.py:87
  42.0 7.2 %fusion.166 = f32[9984,2]{0,1:T(2,128)S(1)} fusion(s32[832]{0:T(1024)S(1)} %get-tuple-element.447, pred[832]{0:T(1024)(128)(4,1)S(1)} %get-tuple-element.448, bf16[832,4,2]{0,2,1:T(2,128)(2,1)S(1)} %dynamic-slice_bitcast_fusion.18), kind=kOutput, calls=%fused_computation.43.clone.1 | convolution fusion | flops 49840128 | bytes 88576 | tf_op jit(solution)/shard_map/while/body/eval_jaxpr/dot_general | solution.py:87
  49.2 7.2 %fusion.167 = f32[9984,2]{0,1:T(2,128)S(1)} fusion(s32[832]{0:T(1024)S(1)} %get-tuple-element.449, pred[832]{0:T(1024)(128)(4,1)S(1)} %get-tuple-element.450, bf16[832,4,2]{0,2,1:T(2,128)(2,1)S(1)} %dynamic-slice_bitcast_fusion.18), kind=kOutput, calls=%fused_computation.44.clone.1 | convolution fusion | flops 49840128 | bytes 88576 | tf_op jit(solution)/shard_map/while/body/eval_jaxpr/dot_general | solution.py:87
  56.4 7.2 %fusion.168 = f32[9984,2]{0,1:T(2,128)S(1)} fusion(s32[832]{0:T(1024)S(1)} %get-tuple-element.451, pred[832]{0:T(1024)(128)(4,1)S(1)} %get-tuple-element.452, bf16[832,4,2]{0,2,1:T(2,128)(2,1)S(1)} %dynamic-slice_bitcast_fusion.18), kind=kOutput, calls=%fused_computation.45.clone.1 | convolution fusion | flops 49840128 | bytes 88576 | tf_op jit(solution)/shard_map/while/body/eval_jaxpr/dot_general | solution.py:87
  63.5 7.2 %fusion.169 = f32[9984,2]{0,1:T(2,128)S(1)} fusion(f32[9984,2]{0,1:T(2,128)S(1)} %fusion.166, f32[9984,2]{0,1:T(2,128)S(1)} %fusion.167, f32[9984,2]{0,1:T(2,128)S(1)} %fusion.168, s32[832]{0:T(1024)S(1)} %get-tuple-element.453, pred[832]{0:T(1024)(128)(4,1)S(1)} %get-tuple-element.454, f32[9984,2]{0,1:T(2,128)S(1)} %get-tuple-element.476, ...), kind=kOutput, calls=%fused_computation.58.clone.1 | convolution fusion | flops 49939968 | bytes 408065 | tf_op jit(solution)/shard_map/while/body/eval_jaxpr/dot_general | solution.py:87
  76.0 15.6 %all_to_all.16 = s32[16,1,624]{2,1,0:T(1,128)S(1)} all-to-all(s32[16,1,624]{2,1,0:T(1,128)S(1)} %sub.28), channel_id=1, replica_groups=mesh['shard'=16,'rep'=2] {'shard'}, dimensions={0} | all-to-all | bytes 79872 | tf_op jit(solution)/shard_map/all_to_all | solution.py:103
  92.2 11.0 %fusion.96 = bf16[16,624,128]{2,1,0:T(8,128)(2,1)} fusion(bf16[832,128,1]{1,0,2:T(8,128)(2,1)S(1)} %bitcast.103, s32[16,624]{1,0:T(8,128)S(1)} %bitcast.105), kind=kOutput, calls=%fused_computation.119 | convolution fusion | flops 2136096768 | bytes 2808832 | tf_op jit(solution)/shard_map/ojk,kt->ojt/dot_general | solution.py:105
  103.3 4.6 %all-to-all-start.1 = ((bf16[16,624,128]{2,1,0:T(8,128)(2,1)}), bf16[16,624,128]{2,1,0:T(8,128)(2,1)}, u32[]{:S(2)}, u32[]{:S(2)}) async-start(bf16[16,624,128]{2,1,0:T(8,128)(2,1)} %fusion.96), calls=%async_computation.1 | async-start | bytes 5111808 | tf_op jit(solution)/shard_map/all_to_all | solution.py:108
  109.2 1.0 convert_element_type.141
  110.9 47.0 %all-to-all-done.1 = bf16[16,624,128]{2,1,0:T(8,128)(2,1)} async-done(((bf16[16,624,128]{2,1,0:T(8,128)(2,1)}), bf16[16,624,128]{2,1,0:T(8,128)(2,1)}, u32[]{:S(2)}, u32[]{:S(2)}) %all-to-all-start.1) | async-done | bytes 2555936 | tf_op jit(solution)/shard_map/all_to_all | solution.py:108
  157.9 57.4 %while.36 = (s32[]{:T(128)}, bf16[2,832,128]{2,1,0:T(8,128)(2,1)}, s32[2,832,4]{1,2,0:T(4,128)S(1)}, pred[2,832,4]{1,2,0:T(4,128)(4,1)S(1)}, bf16[9984,128]{1,0:T(8,128)(2,1)}, /*index=5*/s32[]{:T(128)}) while((s32[]{:T(128)}, bf16[2,832,128]{2,1,0:T(8,128)(2,1)}, s32[2,832,4]{1,2,0:T(4,128)S(1)}, ...), condition=%wide.region_5.6_spmd.clone.clone, body=%wide.region_4.5_spmd.clone.clone.sunk | while | flops 2292645888 | bytes 3065677 | solution.py:121
  158.2 28.2 %fusion.161 = bf16[2,832,128]{2,1,0:T(8,128)(2,1)} fusion(bf16[2,832,128]{2,1,0:T(8,128)(2,1)} %get-tuple-element.496, s32[]{:T(128)} %get-tuple-element.495, bf16[9984,128]{1,0:T(8,128)(2,1)} %get-tuple-element.505, s32[832]{0:T(1024)S(1)} %get-tuple-element.434, s32[832]{0:T(1024)S(1)} %get-tuple-element.435, s32[832]{0:T(1024)S(1)} %get-tuple-element.436, ...), kind=kOutput, calls=%fused_computation.24.clone.1 | convolution fusion | flops 2292645888 | bytes 2999040 | tf_op jit(solution)/shard_map/while/body/eval_jaxpr/dot_general | solution.py:116
  186.6 28.2 %fusion.161 = bf16[2,832,128]{2,1,0:T(8,128)(2,1)} fusion(bf16[2,832,128]{2,1,0:T(8,128)(2,1)} %get-tuple-element.496, s32[]{:T(128)} %get-tuple-element.495, bf16[9984,128]{1,0:T(8,128)(2,1)} %get-tuple-element.505, s32[832]{0:T(1024)S(1)} %get-tuple-element.434, s32[832]{0:T(1024)S(1)} %get-tuple-element.435, s32[832]{0:T(1024)S(1)} %get-tuple-element.436, ...), kind=kOutput, calls=%fused_computation.24.clone.1 | convolution fusion | flops 2292645888 | bytes 2999040 | tf_op jit(solution)/shard_map/while/body/eval_jaxpr/dot_general | solution.py:116
  215.3 1.6 convert_element_type.136
  216.9 3.4 fusion.110
  220.3 3.8 fusion.95
  224.1 1.5 reshape.199
  225.6 70.1 %while.38 = (s32[]{:T(128)}, f32[9984,128]{1,0:T(8,128)}, s32[2,832,4]{1,2,0:T(4,128)S(1)}, pred[2,832,4]{1,2,0:T(4,128)(4,1)S(1)}, bf16[2,832,128]{2,1,0:T(8,128)(2,1)S(1)}, /*index=5*/s32[]{:T(128)}, s32[]{:T(128)}) while((s32[]{:T(128)}, f32[9984,128]{1,0:T(8,128)}, s32[2,832,4]{1,2,0:T(4,128)S(1)}, ...), condition=%wide.region_7.8_spmd.clone.clone, body=%wide.region_6.7_spmd.clone.clone.sunk | while | flops 2295201792 | bytes 10523747 | solution.py:164
  234.3 29.3 %fusion.172 = f32[9984,128]{1,0:T(8,128)} fusion(s32[832]{0:T(1024)S(1)} %get-tuple-element.460, s32[832]{0:T(1024)S(1)} %get-tuple-element.461, s32[832]{0:T(1024)S(1)} %get-tuple-element.462, s32[832]{0:T(1024)S(1)} %get-tuple-element.463, pred[832]{0:T(1024)(128)(4,1)S(1)} %get-tuple-element.464, pred[832]{0:T(1024)(128)(4,1)S(1)} %get-tuple-element.465, ...), kind=kOutput, calls=%fused_computation.98.clone.1 | convolution fusion | flops 2295201792 | bytes 10457093 | tf_op jit(solution)/shard_map/while/body/eval_jaxpr/dot_general | solution.py:155
  263.7 31.8 %fusion.172 = f32[9984,128]{1,0:T(8,128)} fusion(s32[832]{0:T(1024)S(1)} %get-tuple-element.460, s32[832]{0:T(1024)S(1)} %get-tuple-element.461, s32[832]{0:T(1024)S(1)} %get-tuple-element.462, s32[832]{0:T(1024)S(1)} %get-tuple-element.463, pred[832]{0:T(1024)(128)(4,1)S(1)} %get-tuple-element.464, pred[832]{0:T(1024)(128)(4,1)S(1)} %get-tuple-element.465, ...), kind=kOutput, calls=%fused_computation.98.clone.1 | convolution fusion | flops 2295201792 | bytes 10457093 | tf_op jit(solution)/shard_map/while/body/eval_jaxpr/dot_general | solution.py:155
  295.7 2.6 convert_element_type.145
  298.3 69.6 %all_to_all.17 = bf16[16,624,128]{2,1,0:T(8,128)(2,1)S(1)} all-to-all(bf16[16,624,128]{2,1,0:T(8,128)(2,1)S(1)} %bitcast.101), channel_id=1, replica_groups=mesh['shard'=16,'rep'=2] {'shard'}, dimensions={0} | all-to-all | bytes 5111808 | tf_op jit(solution)/shard_map/all_to_all | solution.py:170
  367.9 9.0 %fusion.101 = bf16[832,128]{1,0:T(8,128)(2,1)} fusion(bf16[16,624,128]{2,1,0:T(8,128)(2,1)S(1)} %all_to_all.17, s32[16,624]{1,0:T(8,128)S(1)} %bitcast.106), kind=kOutput, calls=%fused_computation.126 | convolution fusion | flops 2134925312 | bytes 2808832 | tf_op jit(solution)/shard_map/jbp,jbm->pm/dot_general | solution.py:172
  378.3 4.7 %reduce-scatter.2.cloned.1.call-done = bf16[416,128]{1,0:T(8,128)(2,1)} async-done(((bf16[832,128]{1,0:T(8,128)(2,1)}), bf16[416,128]{1,0:T(8,128)(2,1)}) %reduce-scatter.2.cloned.1.call-update) | async-done | bytes 106512 | tf_op jit(solution)/shard_map/reduce_scatter | solution.py:176
  383.0 1.0 fusion.116
  384.2 1.0 fusion.118
  385.2 2.0 all_gather.6
  388.1 2.4 all-reduce
  (102 shorter events, 11.5 us)
Async XLA Ops:
  7.2 209.7 %copy-start = (bf16[512,1792]{1,0:T(8,128)(2,1)S(1)}, bf16[512,1792]{1,0:T(8,128)(2,1)}, u32[]{:S(2)}) copy-start(bf16[512,1792]{1,0:T(8,128)(2,1)} %param.27) | copy-start | bytes 5505028
  12.7 79.5 %copy-start.6 = (bf16[13,64,128]{2,1,0:T(8,128)(2,1)S(1)}, bf16[13,64,128]{2,1,0:T(8,128)(2,1)}, u32[]{:S(2)}) copy-start(bf16[13,64,128]{2,1,0:T(8,128)(2,1)} %param.24) | copy-start | bytes 638980
  91.6 0.6 copy-start.8
  103.2 4.7 %copy-start.4 = (bf16[512,256]{1,0:T(8,128)(2,1)S(1)}, bf16[512,256]{1,0:T(8,128)(2,1)}, u32[]{:S(2)}) copy-start(bf16[512,256]{1,0:T(8,128)(2,1)} %param.22) | copy-start | bytes 786436
  103.2 4.7 %copy-start.12 = (bf16[13,512]{1,0:T(8,128)(2,1)S(1)}, bf16[13,512]{1,0:T(8,128)(2,1)}, u32[]{:S(2)}) copy-start(bf16[13,512]{1,0:T(8,128)(2,1)} %param.21) | copy-start | bytes 39940
  103.2 4.7 %copy-start.15 = (bf16[128,13]{0,1:T(8,128)(2,1)S(1)}, bf16[128,13]{0,1:T(8,128)(2,1)}, u32[]{:S(2)}) copy-start(bf16[128,13]{0,1:T(8,128)(2,1)} %param.18) | copy-start | bytes 9988
  103.2 5.1 %copy-start.5 = (bf16[256,128]{1,0:T(8,128)(2,1)S(1)}, bf16[256,128]{1,0:T(8,128)(2,1)}, u32[]{:S(2)}) copy-start(bf16[256,128]{1,0:T(8,128)(2,1)} %param.23) | copy-start | bytes 196612
  103.2 6.0 %copy-start.2 = (bf16[128,1792]{1,0:T(8,128)(2,1)S(1)}, bf16[128,1792]{1,0:T(8,128)(2,1)}, u32[]{:S(2)}) copy-start(bf16[128,1792]{1,0:T(8,128)(2,1)} %param.29) | copy-start | bytes 1376260
  103.2 7.0 %copy-start.10 = (f32[1792]{0:T(1024)S(1)}, f32[1792]{0:T(1024)}, u32[]{:S(2)}) copy-start(f32[1792]{0:T(1024)} %param.28) | copy-start | bytes 21508
  103.3 54.6 %all-to-all-start.1 = ((bf16[16,624,128]{2,1,0:T(8,128)(2,1)}), bf16[16,624,128]{2,1,0:T(8,128)(2,1)}, u32[]{:S(2)}, u32[]{:S(2)}) async-start(bf16[16,624,128]{2,1,0:T(8,128)(2,1)} %fusion.96), calls=%async_computation.1 | async-start | bytes 5111808 | tf_op jit(solution)/shard_map/all_to_all | solution.py:108
  107.8 275.2 %reduce-scatter.2.cloned.1.call-start = ((), (), s32[]{:S(2)}) async-start(), calls=%async_computation.4 | async-start | bytes 319488 | tf_op jit(solution)/shard_map/reduce_scatter | solution.py:176
  157.9 59.0 %copy-start.3 = (bf16[128,128]{1,0:T(8,128)(2,1)S(1)}, bf16[128,128]{1,0:T(8,128)(2,1)}, u32[]{:S(2)}) copy-start(bf16[128,128]{1,0:T(8,128)(2,1)} %copy.37) | copy-start | bytes 98308
  157.9 59.0 %copy-start.11 = (f32[1792]{0:T(1024)S(1)}, f32[1792]{0:T(1024)}, u32[]{:S(2)}) copy-start(f32[1792]{0:T(1024)} %param.28) | copy-start | bytes 21508
  215.3 5.0 %copy-start.1 = (f32[128,1792]{1,0:T(8,128)S(1)}, f32[128,1792]{1,0:T(8,128)}, u32[]{:S(2)}) copy-start(f32[128,1792]{1,0:T(8,128)} %convert_element_type.141) | copy-start | bytes 2752516
  215.3 5.0 %copy-start.14 = (f32[1664]{0:T(1024)S(1)}, f32[1664]{0:T(1024)}, u32[]{:S(2)}) copy-start(f32[1664]{0:T(1024)} %slice.106) | copy-start | bytes 19972
  295.7 72.3 %copy-start.9 = (s32[16,1,624]{2,0,1:T(8,128)S(1)}, s32[16,1,624]{2,0,1:T(8,128)}, u32[]{:S(2)}) copy-start(s32[16,1,624]{2,0,1:T(8,128)} %copy-done.8) | copy-start | bytes 119812
  367.9 9.1 %copy-start.13 = (f32[13,64]{1,0:T(8,128)S(1)}, f32[13,64]{1,0:T(8,128)}, u32[]{:S(2)}) copy-start(f32[13,64]{1,0:T(8,128)} %param.25) | copy-start | bytes 9988
  367.9 9.1 %copy-start.16 = (u32[32]{0:T(128)S(1)}, u32[32]{0:T(128)}, u32[]{:S(2)}) copy-start(u32[32]{0:T(128)} %constant.110) | copy-start | bytes 388
  367.9 16.2 %copy-start.7 = (bf16[13,64,128]{2,1,0:T(8,128)(2,1)S(1)}, bf16[13,64,128]{2,1,0:T(8,128)(2,1)}, u32[]{:S(2)}) copy-start(bf16[13,64,128]{2,1,0:T(8,128)(2,1)} %param.24) | copy-start | bytes 638980
Sparse Core Ops, SparseCore 0:
  377.1 5.8 reduce-scatter.1
where the time goes:
time: 402 us; the launch traced here: 398 us
  matrix products  203 us (50%)
  blocking collectives  89.6 us (22%)
  waiting for transfers between devices  51.7 us (13%)
  between operations  15.4 us (4%)
  loops' own time  14.8 us (4%)
  local copies, waits for them, and re-layouts  11.1 us (3%)
  other arithmetic  8.1 us (2%)
  starting transfers between devices  4.63 us (1%)
    all_to_all x1, blocking collectives, per_device(): lax.all_to_all(send_grads, 'shard', split_axis=0, concat_axis=0, tiled=True)  69.6 us
    dot_general x2, matrix products, spread_block(): lax.dot_general(bag_marks(dest_part, live_part), grad_part, contract_firs...  61.1 us
    dot_general x8, matrix products, add_ids(): lax.dot_general(slot_marks(dest_part, live_part, slot), digit_part[:, slo...  57.3 us
    dot_general x2, matrix products, pool_block(): jnp.dot(bag_marks(dest_part, live_part), returned_flat, preferred_element...  56.4 us
    all_to_all x1, waiting for transfers between devices, per_device(): lax.all_to_all(picked, 'shard', split_axis=0, concat_axis=0, tiled=True)  47 us
    all_to_all x1, blocking collectives, per_device(): lax.all_to_all(send_ids, 'shard', split_axis=0, concat_axis=0, tiled=True)  15.6 us
    dot_general x1, matrix products, per_device(): jnp.einsum('ojk,kt->ojt', row_flags, table_rows_flat, preferred_element_t...  11 us
    dot_general x1, matrix products, per_device(): jnp.einsum('jbp,jbm->pm', target_flags, received_rows, preferred_element_...  9.02 us
  transfers between devices with their start and end apart: 2, of which 2 were waited for; matrix products, arithmetic and copies ran while one was open for 1% of the time, Pallas kernels for 0%

commit v1 on v0

v1 whole, which is shorter than its diff:
```python
import functools

import jax
import jax.numpy as jnp
from jax import lax
from jax.experimental import pallas as pl
from jax.experimental.pallas import tpu as pltpu
from jax.sharding import PartitionSpec as P

step_size = 1.0
adagrad_eps = 1e-08
contract_last = (((1,), (1,)), ((), ()))


def step_kernel(
    table_count,
    emb_width,
    id_columns,
    id_rows,
    table_block,
    dense,
    w1,
    w2,
    w3,
    cross_down,
    cross_up,
    cross_bias,
    cotangent,
    crossed,
    partial,
    stacked,
    pooled_grad,
):
    step = pl.program_id(0)
    shards, _, rows_dev, _ = table_block.shape
    samples, features = cotangent.shape
    pool_slots = id_columns.shape[2]
    group = min(shards, 16)
    chunk = group * rows_dev

    @pl.when(step < table_count)
    def _lookup():
        ids = id_columns[0]
        total = jnp.zeros((samples, emb_width), jnp.float32)
        for first in range(0, shards, group):
            names = lax.broadcasted_iota(jnp.int32, (samples, chunk), 1) + first * rows_dev
            counts = jnp.zeros((samples, chunk), jnp.float32)
            for slot in range(pool_slots):
                counts = counts + jnp.where(names == ids[:, slot : slot + 1], 1.0, 0.0)
            rows = table_block[first : first + group, 0].reshape(chunk, emb_width)
            total = total + jnp.dot(
                counts.astype(jnp.bfloat16), rows, preferred_element_type=jnp.float32
            )
        place = pl.multiple_of((step + 1) * emb_width, emb_width)
        stacked[:, pl.ds(place, emb_width)] = total.astype(jnp.bfloat16)

    @pl.when(step == table_count - 1)
    def _cross():
        def layer(x, w):
            return jax.nn.relu(jnp.dot(x, w[...], preferred_element_type=jnp.float32)).astype(
                jnp.bfloat16
            )

        stacked[:, :emb_width] = layer(layer(layer(dense[...], w1), w2), w3)
        low_rank = jnp.dot(
            stacked[...], cross_down[...], preferred_element_type=jnp.float32
        ).astype(jnp.bfloat16)
        hidden_grad = (
            cotangent[...].astype(jnp.float32) * stacked[...].astype(jnp.float32)
        ).astype(jnp.bfloat16)
        low_grad = lax.dot_general(
            hidden_grad, cross_up[...], contract_last, preferred_element_type=jnp.float32
        ).astype(jnp.bfloat16)
        width = 2 * emb_width if features % (2 * emb_width) == 0 else emb_width
        for start in range(0, features, width):
            part = slice(start, start + width)
            hidden = (
                jnp.dot(low_rank, cross_up[:, part], preferred_element_type=jnp.float32)
                + cross_bias[:, part]
            )
            wide = stacked[:, part].astype(jnp.float32)
            crossed[:, part] = (wide * hidden + wide).astype(jnp.bfloat16)
            back = lax.dot_general(
                low_grad, cross_down[part, :], contract_last, preferred_element_type=jnp.float32
            )
            grad = cotangent[:, part].astype(jnp.float32) * (hidden + 1.0) + back
            for inner in range(0, width, emb_width):
                table = (start + inner) // emb_width - 1
                if table >= 0:
                    pooled_grad[table] = grad[:, inner : inner + emb_width].astype(jnp.bfloat16)

    @pl.when(step >= table_count)
    def _spread():
        ids = id_rows[0]
        grad = pooled_grad[step - table_count]
        for first in range(0, shards, group):
            names = lax.broadcasted_iota(jnp.int32, (chunk, samples), 0) + first * rows_dev
            counts = jnp.zeros((chunk, samples), jnp.float32)
            for slot in range(pool_slots):
                counts = counts + jnp.where(names == ids[slot : slot + 1, :], 1.0, 0.0)
            sums = jnp.dot(counts.astype(jnp.bfloat16), grad, preferred_element_type=jnp.float32)
            partial[first : first + group, 0] = sums.astype(jnp.bfloat16).reshape(
                group, rows_dev, emb_width
            )


def per_device(
    dense_feats,
    lookup_ids,
    bag_lengths,
    bottom_w1,
    bottom_w2,
    bottom_w3,
    tables,
    accum,
    cross_down,
    cross_up,
    cross_bias,
    cotangent,
):
    shards = lax.axis_size("shard")
    reps = lax.axis_size("rep")
    samples, table_count, pool_slots = lookup_ids.shape
    rows_dev, emb_width = tables.shape[1:]
    features = cotangent.shape[1]
    gathered = lax.all_gather(tables, "shard", axis=0, tiled=False)
    live_mask = jnp.arange(pool_slots, dtype=jnp.int32)[None, None, :] < bag_lengths[:, :, None]
    coded = jnp.where(live_mask, lookup_ids, -1)
    id_columns = coded.transpose(1, 0, 2)
    id_rows = coded.transpose(1, 2, 0)

    def whole(array):
        return pl.BlockSpec(array.shape, lambda i: (0,) * array.ndim)

    bias = cross_bias[None, :]
    last = table_count - 1
    crossed, partial = pl.pallas_call(
        functools.partial(step_kernel, table_count, emb_width),
        grid=(2 * table_count,),
        in_specs=[
            pl.BlockSpec((1, samples, pool_slots), lambda i: (jnp.minimum(i, last), 0, 0)),
            pl.BlockSpec(
                (1, pool_slots, samples), lambda i: (jnp.maximum(i - table_count, 0), 0, 0)
            ),
            pl.BlockSpec(
                (shards, 1, rows_dev, emb_width), lambda i: (0, jnp.minimum(i, last), 0, 0)
            ),
            whole(dense_feats),
            whole(bottom_w1),
            whole(bottom_w2),
            whole(bottom_w3),
            whole(cross_down),
            whole(cross_up),
            whole(bias),
            whole(cotangent),
        ],
        out_specs=[
            pl.BlockSpec((samples, features), lambda i: (0, 0)),
            pl.BlockSpec(
                (shards, 1, rows_dev, emb_width),
                lambda i: (0, jnp.maximum(i - table_count, 0), 0, 0),
            ),
        ],
        out_shape=[
            jax.ShapeDtypeStruct((samples, features), jnp.bfloat16),
            jax.ShapeDtypeStruct((shards, table_count, rows_dev, emb_width), jnp.bfloat16),
        ],
        scratch_shapes=[
            pltpu.VMEM((samples, features), jnp.bfloat16),
            pltpu.VMEM((table_count, samples, emb_width), jnp.bfloat16),
        ],
        compiler_params=pltpu.CompilerParams(
            dimension_semantics=("arbitrary",), vmem_limit_bytes=40 * 2**20
        ),
    )(
        id_columns,
        id_rows,
        gathered,
        dense_feats,
        bottom_w1,
        bottom_w2,
        bottom_w3,
        cross_down,
        cross_up,
        bias,
        cotangent,
    )
    received = lax.all_to_all(partial, "shard", split_axis=0, concat_axis=0, tiled=True)
    group_grad = jnp.sum(received.astype(jnp.float32), axis=0).astype(jnp.bfloat16)
    row_grad = group_grad.astype(jnp.float32)
    shifted = group_grad
    for _ in range(reps - 1):
        shifted = lax.ppermute(shifted, "rep", [(r, (r + 1) % reps) for r in range(reps)])
        row_grad = row_grad + shifted.astype(jnp.float32)
    new_accum = accum + jnp.mean(row_grad * row_grad, axis=2)
    new_tables = tables.astype(jnp.float32) - step_size * row_grad / (
        jnp.sqrt(new_accum)[:, :, None] + adagrad_eps
    )
    return (crossed, new_tables, new_accum)


def solution(mesh):
    in_specs = (
        P(("shard", "rep"), None),
        P(("shard", "rep"), None, None),
        P(("shard", "rep"), None),
        P(),
        P(),
        P(),
        P(None, "shard", None),
        P(None, "shard"),
        P(),
        P(),
        P(),
        P(("shard", "rep"), None),
    )
    out_specs = (P(("shard", "rep"), None), P(None, "shard", None), P(None, "shard"))
    return jax.shard_map(
        per_device, mesh=mesh, in_specs=in_specs, out_specs=out_specs, check_vma=False
    )
```

time: 402 us -> 201 us (0.50)
  matrix products: 203 us -> 0 us
  waiting for transfers between devices: 51.7 us -> 74.9 us
  loops' own time: 14.8 us -> 0 us
  Pallas kernels: 0 us -> 14.6 us
  blocking collectives: 89.6 us -> 80.8 us
  starting transfers between devices: 4.63 us -> 0.04 us
    dot_general x20 -> x0, matrix products: 203 us -> none  [the longest x2 61.1 us: spread_block(): lax.dot_general(bag_marks(dest_part, live_part), grad_part, contract_firs...]
    all_gather x0 -> x1, waiting for transfers between devices: none -> 72.5 us  [per_device(): gathered = lax.all_gather(tables, 'shard', axis=0, tiled=False)]
    all_to_all x1 -> x0, waiting for transfers between devices: 47 us -> none  [per_device(): lax.all_to_all(picked, 'shard', split_axis=0, concat_axis=0, tiled=True)]
    another operation x3 -> x0, loops' own time: 14.8 us -> none  [the longest x1 8.76 us: per_device(): lax.scan(spread_block, jnp.zeros((send_width, emb_width), jnp.float32), (...]
    pallas_call x0 -> x1, Pallas kernels: none -> 14.6 us  [per_device(): pl.pallas_call(functools.partial(step_kernel, table_count, emb_width), gr...]
    unnamed x41 -> x17, local copies, waits for them, and re-layouts: 2.29 us -> 9.3 us
    convert_element_type x6 -> x0, other arithmetic: 4.81 us -> none  [the longest x1 2.65 us: per_device(): spread.astype(jnp.bfloat16).reshape(shards, capacity, emb_width)]
    reduce_scatter x1 -> x0, waiting for transfers between devices: 4.7 us -> none  [per_device(): lax.psum_scatter(group_grad.astype(jnp.bfloat16), 'rep', scatter_dimensio...]
where the time goes in v1:
time: 201 us
  blocking collectives  80.8 us (40%)
  waiting for transfers between devices  74.9 us (37%)
  Pallas kernels  14.6 us (7%)
  between operations  14.1 us (7%)
  local copies, waits for them, and re-layouts  10.3 us (5%)
  other arithmetic  5.87 us (3%)
    all_to_all x1, blocking collectives, per_device(): lax.all_to_all(partial, 'shard', split_axis=0, concat_axis=0, tiled=True)  80.8 us
    all_gather x1, waiting for transfers between devices, per_device(): gathered = lax.all_gather(tables, 'shard', axis=0, tiled=False)  72.5 us
    pallas_call x1, Pallas kernels, per_device(): pl.pallas_call(functools.partial(step_kernel, table_count, emb_width), gr...  14.6 us
    unnamed x17, local copies, waits for them, and re-layouts  9.3 us
  transfers between devices with their start and end apart: 2, of which 2 were waited for; matrix products, arithmetic and copies ran while one was open for 1% of the time, Pallas kernels for 0%

profile of v1, /device:TPU:0, one launch (start us, length us, event | category | flops | bytes accessed | tf_op | source)
XLA Modules:
  0.0 200.6 jit_solution(12774989576998949005)
XLA Ops:
  7.2 0.0 all-gather.3.cloned.1.call-start
  7.2 0.7 all-gather.3.cloned.1.call-update
  7.9 0.7 broadcast_in_dim.11.cross_bias
  8.6 0.8 copy.18.dense
  9.4 0.8 fusion.1
  10.2 0.3 copy.17.id_columns
  10.5 72.5 %all-gather.3.cloned.1.call-done = bf16[208,64,128]{2,1,0:T(8,128)(2,1)} async-done(((bf16[13,64,128]{2,1,0:T(8,128)(2,1)}), bf16[208,64,128]{2,1,0:T(8,128)(2,1)}) %all-gather.3.cloned.1.call-update) | async-done | bytes 3407888 | tf_op jit(solution)/shard_map/all_gather | solution.py:126
  83.0 0.0 copy-start
  83.0 2.0 copy-done
  85.0 0.0 copy-start.1
  85.0 1.5 copy-done.1
  86.5 0.0 copy-start.2
  86.5 1.5 copy-done.2
  88.0 0.0 copy-start.3
  88.0 1.0 copy-done.3
  89.0 0.0 copy-start.4
  89.0 0.9 copy-done.4
  90.0 0.0 copy-start.5
  90.0 0.8 copy-done.5
  90.8 0.0 copy-start.6
  90.8 0.7 copy-done.6
  91.5 14.6 %shard_map.139 = (bf16[128,1792]{1,0:T(8,128)(2,1)}, bf16[16,13,64,128]{3,2,1,0:T(8,128)(2,1)S(1)}) custom-call(s32[13,128,4]{2,1,0:T(8,128)S(1)} %copy.17.id_columns, s32[13,4,128]{2,1,0:T(4,128)S(1)} %get-tuple-element.9.id_rows, bf16[16,13,64,128]{3,2,1,0:T(8,128)(2,1)S(1)} %bitcast.5, bf16[128,13]{1,0:T(8,128)(2,1)S(1)} %copy.18.dense, ...), custom_call_target="tpu_custom_call" | custom-call | tf_op jit(solution)/shard_map/pallas_call | solution.py:137
  106.2 80.8 %all_to_all.5 = bf16[16,13,64,128]{3,2,1,0:T(8,128)(2,1)S(1)} all-to-all(bf16[16,13,64,128]{3,2,1,0:T(8,128)(2,1)S(1)} %get-tuple-element.6), channel_id=1, replica_groups=mesh['shard'=16,'rep'=2] {'shard'}, dimensions={0} | all-to-all | bytes 6815744 | tf_op jit(solution)/shard_map/all_to_all | solution.py:188
  186.9 0.0 copy-start.7
  187.0 1.4 reduce_sum.21
  188.4 0.0 collective-permute-start
  188.4 1.7 collective-permute-done
  190.0 1.1 multiply_reduce_fusion
  191.2 0.0 copy-done.7
  191.2 0.6 sqrt_add_fusion
  191.8 2.0 divide_subtract_fusion
Async XLA Ops:
  7.2 75.9 %all-gather.3.cloned.1.call-start = ((), (), s32[]{:S(2)}) async-start(), calls=%async_computation.1 | async-start | bytes 3620864 | tf_op jit(solution)/shard_map/all_gather | solution.py:126
  83.0 2.0 copy-start
  85.0 1.5 copy-start.1
  86.5 1.5 copy-start.2
  88.0 1.0 copy-start.3
  89.0 0.9 copy-start.4
  90.0 0.8 copy-start.5
  90.8 0.7 copy-start.6
  186.9 4.2 %copy-start.7 = (f32[13,64]{1,0:T(8,128)S(1)}, f32[13,64]{1,0:T(8,128)}, u32[]{:S(2)}) copy-start(f32[13,64]{1,0:T(8,128)} %param.19) | copy-start | bytes 9988
  188.4 1.7 collective-permute-start
Sparse Core Ops, SparseCore 0:
  10.7 72.3 all-gather.2

commit v2 on v1

--- a/solution.py
+++ b/solution.py
@@ -15,9 +15,9 @@
 def step_kernel(
     table_count,
     emb_width,
+    reps,
     id_columns,
     id_rows,
-    table_block,
     dense,
     w1,
     w2,
@@ -26,13 +26,13 @@
     cross_up,
     cross_bias,
     cotangent,
-    crossed,
-    partial,
-    stacked,
-    pooled_grad,
+    *refs,
 ):
+    table_blocks, (crossed, *partials) = refs[:reps], refs[reps : 2 * reps + 1]
+    stacked, pooled_grad = refs[2 * reps + 1 :]
     step = pl.program_id(0)
-    shards, _, rows_dev, _ = table_block.shape
+    shards, _, rows_dev, _ = table_blocks[0].shape
+    pieces = [(turn, first) for turn in range(reps) for first in range(0, shards, min(shards, 16))]
     samples, features = cotangent.shape
     pool_slots = id_columns.shape[2]
     group = min(shards, 16)
@@ -42,12 +42,13 @@
     def _lookup():
         ids = id_columns[0]
         total = jnp.zeros((samples, emb_width), jnp.float32)
-        for first in range(0, shards, group):
-            names = lax.broadcasted_iota(jnp.int32, (samples, chunk), 1) + first * rows_dev
+        for turn, first in pieces:
+            begin = (turn * shards + first) * rows_dev
+            names = lax.broadcasted_iota(jnp.int32, (samples, chunk), 1) + begin
             counts = jnp.zeros((samples, chunk), jnp.float32)
             for slot in range(pool_slots):
                 counts = counts + jnp.where(names == ids[:, slot : slot + 1], 1.0, 0.0)
-            rows = table_block[first : first + group, 0].reshape(chunk, emb_width)
+            rows = table_blocks[turn][first : first + group, 0].reshape(chunk, emb_width)
             total = total + jnp.dot(
                 counts.astype(jnp.bfloat16), rows, preferred_element_type=jnp.float32
             )
@@ -93,13 +94,14 @@
     def _spread():
         ids = id_rows[0]
         grad = pooled_grad[step - table_count]
-        for first in range(0, shards, group):
-            names = lax.broadcasted_iota(jnp.int32, (chunk, samples), 0) + first * rows_dev
+        for turn, first in pieces:
+            begin = (turn * shards + first) * rows_dev
+            names = lax.broadcasted_iota(jnp.int32, (chunk, samples), 0) + begin
             counts = jnp.zeros((chunk, samples), jnp.float32)
             for slot in range(pool_slots):
                 counts = counts + jnp.where(names == ids[slot : slot + 1, :], 1.0, 0.0)
             sums = jnp.dot(counts.astype(jnp.bfloat16), grad, preferred_element_type=jnp.float32)
-            partial[first : first + group, 0] = sums.astype(jnp.bfloat16).reshape(
+            partials[turn][first : first + group, 0] = sums.astype(jnp.bfloat16).reshape(
                 group, rows_dev, emb_width
             )
 
@@ -123,9 +125,20 @@
     samples, table_count, pool_slots = lookup_ids.shape
     rows_dev, emb_width = tables.shape[1:]
     features = cotangent.shape[1]
-    gathered = lax.all_gather(tables, "shard", axis=0, tiled=False)
+    me = lax.axis_index("rep")
+    half = rows_dev // reps
+
+    def shift(array, by):
+        return lax.ppermute(array, "rep", [(r, (r + by) % reps) for r in range(reps)])
+
+    own_rows = lax.dynamic_slice_in_dim(tables, me * half, half, axis=1)
+    own_gathered = lax.all_gather(own_rows, "shard", axis=0, tiled=False)
+    gathered = [own_gathered] + [shift(own_gathered, -turn) for turn in range(1, reps)]
     live_mask = jnp.arange(pool_slots, dtype=jnp.int32)[None, None, :] < bag_lengths[:, :, None]
-    coded = jnp.where(live_mask, lookup_ids, -1)
+    within = lookup_ids % rows_dev
+    turns = (within // half - me + reps) % reps
+    places = (turns * shards + lookup_ids // rows_dev) * half + within % half
+    coded = jnp.where(live_mask, places, -1)
     id_columns = coded.transpose(1, 0, 2)
     id_rows = coded.transpose(1, 2, 0)
 
@@ -134,16 +147,13 @@
 
     bias = cross_bias[None, :]
     last = table_count - 1
-    crossed, partial = pl.pallas_call(
-        functools.partial(step_kernel, table_count, emb_width),
+    crossed, *partials = pl.pallas_call(
+        functools.partial(step_kernel, table_count, emb_width, reps),
         grid=(2 * table_count,),
         in_specs=[
             pl.BlockSpec((1, samples, pool_slots), lambda i: (jnp.minimum(i, last), 0, 0)),
             pl.BlockSpec(
                 (1, pool_slots, samples), lambda i: (jnp.maximum(i - table_count, 0), 0, 0)
-            ),
-            pl.BlockSpec(
-                (shards, 1, rows_dev, emb_width), lambda i: (0, jnp.minimum(i, last), 0, 0)
             ),
             whole(dense_feats),
             whole(bottom_w1),
@@ -153,18 +163,23 @@
             whole(cross_up),
             whole(bias),
             whole(cotangent),
-        ],
+        ]
+        + [pl.BlockSpec((shards, 1, half, emb_width), lambda i: (0, jnp.minimum(i, last), 0, 0))]
+        * reps,
         out_specs=[
             pl.BlockSpec((samples, features), lambda i: (0, 0)),
+        ]
+        + [
             pl.BlockSpec(
-                (shards, 1, rows_dev, emb_width),
+                (shards, 1, half, emb_width),
                 lambda i: (0, jnp.maximum(i - table_count, 0), 0, 0),
-            ),
-        ],
+            )
+        ]
+        * reps,
         out_shape=[
             jax.ShapeDtypeStruct((samples, features), jnp.bfloat16),
-            jax.ShapeDtypeStruct((shards, table_count, rows_dev, emb_width), jnp.bfloat16),
-        ],
+        ]
+        + [jax.ShapeDtypeStruct((shards, table_count, half, emb_width), jnp.bfloat16)] * reps,
         scratch_shapes=[
             pltpu.VMEM((samples, features), jnp.bfloat16),
             pltpu.VMEM((table_count, samples, emb_width), jnp.bfloat16),
@@ -175,7 +190,6 @@
     )(
         id_columns,
         id_rows,
-        gathered,
         dense_feats,
         bottom_w1,
         bottom_w2,
@@ -184,14 +198,21 @@
         cross_up,
         bias,
         cotangent,
-    )
-    received = lax.all_to_all(partial, "shard", split_axis=0, concat_axis=0, tiled=True)
-    group_grad = jnp.sum(received.astype(jnp.float32), axis=0).astype(jnp.bfloat16)
-    row_grad = group_grad.astype(jnp.float32)
-    shifted = group_grad
-    for _ in range(reps - 1):
-        shifted = lax.ppermute(shifted, "rep", [(r, (r + 1) % reps) for r in range(reps)])
-        row_grad = row_grad + shifted.astype(jnp.float32)
+        *gathered,
+    )
+    chip_sum = partials[0].astype(jnp.float32)
+    for turn in range(1, reps):
+        chip_sum = chip_sum + shift(partials[turn], turn).astype(jnp.float32)
+    received = lax.all_to_all(
+        chip_sum.astype(jnp.bfloat16), "shard", split_axis=0, concat_axis=0, tiled=True
+    )
+    own_grad = jnp.sum(received.astype(jnp.float32), axis=0)
+    row_grad = jnp.zeros((table_count, rows_dev, emb_width), jnp.float32)
+    for turn in range(reps):
+        piece = shift(own_grad, -turn) if turn else own_grad
+        row_grad = lax.dynamic_update_slice_in_dim(
+            row_grad, piece, (me + turn) % reps * half, axis=1
+        )
     new_accum = accum + jnp.mean(row_grad * row_grad, axis=2)
     new_tables = tables.astype(jnp.float32) - step_size * row_grad / (
         jnp.sqrt(new_accum)[:, :, None] + adagrad_eps

time: 201 us -> 159 us (0.79)
  blocking collectives: 80.8 us -> 45.7 us
  waiting for transfers between devices: 74.9 us -> 68.9 us
    all_to_all x1, blocking collectives: 80.8 us -> 45.7 us  [per_device(): lax.all_to_all(chip_sum.astype(jnp.bfloat16), 'shard', split_axis=0, conc...]
    all_gather x1, waiting for transfers between devices: 72.5 us -> 64.1 us  [per_device(): own_gathered = lax.all_gather(own_rows, 'shard', axis=0, tiled=False)]
    ppermute x1 -> x3, waiting for transfers between devices: 1.67 us -> 4.83 us  [shift(): lax.ppermute(array, 'rep', [(r, (r + by) % reps) for r in range(reps)])]
    unnamed x17 -> x19, local copies, waits for them, and re-layouts: 9.3 us -> 7.79 us
  transfers between devices with their start and end apart: 2 -> 4, of which waited for: 2 -> 4; matrix products, arithmetic and copies ran while one was open for 1% -> 2% of each run, Pallas kernels for 0% -> 0%
where the time goes in v2:
time: 159 us; the launch traced here: 158 us
  waiting for transfers between devices  68.9 us (43%)
  blocking collectives  45.7 us (29%)
  Pallas kernels  14.7 us (9%)
  between operations  14.1 us (9%)
  local copies, waits for them, and re-layouts  10.5 us (7%)
  other arithmetic  4.17 us (3%)
    all_gather x1, waiting for transfers between devices, per_device(): own_gathered = lax.all_gather(own_rows, 'shard', axis=0, tiled=False)  64.1 us
    all_to_all x1, blocking collectives, per_device(): lax.all_to_all(chip_sum.astype(jnp.bfloat16), 'shard', split_axis=0, conc...  45.7 us
    pallas_call x1, Pallas kernels, per_device(): pl.pallas_call(functools.partial(step_kernel, table_count, emb_width, rep...  14.7 us
    unnamed x19, local copies, waits for them, and re-layouts  7.79 us
    ppermute x3, waiting for transfers between devices, shift(): lax.ppermute(array, 'rep', [(r, (r + by) % reps) for r in range(reps)])  4.83 us
  transfers between devices with their start and end apart: 4, of which 4 were waited for; matrix products, arithmetic and copies ran while one was open for 2% of the time, Pallas kernels for 0%

profile of v2, /device:TPU:0, one launch (start us, length us, event | category | flops | bytes accessed | tf_op | source)
XLA Modules:
  0.0 158.5 jit_solution(14039424225893182323)
XLA Ops:
  7.2 0.0 copy-start.3
  7.2 0.0 all-gather.3.cloned.1.call-start
  7.2 1.6 %constant_dynamic-slice_fusion = bf16[13,32,128]{2,1,0:T(8,128)(2,1)} fusion(bf16[13,64,128]{2,1,0:T(8,128)(2,1)} %param.18, s32[]{:T(128)S(6)} %select_n.52), kind=kLoop, calls=%fused_computation.35 | loop fusion | bytes 212996 | tf_op jit(solution)/shard_map/dynamic_slice | solution.py:134
  8.8 0.0 all-gather.3.cloned.1.call-update
  8.8 64.1 %all-gather.3.cloned.1.call-done = bf16[208,32,128]{2,1,0:T(8,128)(2,1)} async-done(((bf16[13,32,128]{2,1,0:T(8,128)(2,1)}), bf16[208,32,128]{2,1,0:T(8,128)(2,1)}) %all-gather.3.cloned.1.call-update) | async-done | bytes 1703952 | tf_op jit(solution)/shard_map/all_gather | solution.py:135
  72.9 0.0 collective-permute-start
  72.9 0.9 fusion.12
  73.8 0.3 copy.17.id_columns
  74.1 0.8 copy.18.dense
  75.0 0.7 broadcast_in_dim.6.cross_bias
  75.7 0.9 fusion.11.id_rows
  76.5 0.2 collective-permute-done.refs_1_
  76.7 0.0 copy-done.3
  76.7 1.5 copy-done
  78.2 1.5 copy-done.1
  79.7 1.5 copy-done.2
  81.2 0.9 copy-done.4
  82.2 0.8 copy-done.5
  83.0 0.7 copy-done.6
  83.7 14.7 %shard_map.139 = (bf16[128,1792]{1,0:T(8,128)(2,1)}, bf16[16,13,32,128]{3,2,1,0:T(8,128)(2,1)S(1)}, bf16[16,13,32,128]{3,2,1,0:T(8,128)(2,1)S(1)}) custom-call(s32[13,128,4]{2,1,0:T(8,128)S(1)} %copy.17.id_columns, s32[13,4,128]{2,1,0:T(4,128)S(1)} %fusion.11.id_rows, bf16[128,13]{1,0:T(8,128)(2,1)S(1)} %copy.18.dense, bf16[13,512]{1,0:T(8,128)(2,1)S(1)} %copy-done.6, ...), custom_call_target="tpu_custom_call" | custom-call | tf_op jit(solution)/shard_map/pallas_call | solution.py:150
  98.4 0.3 collective-permute-start.1
  98.7 3.3 %collective-permute-done.1 = bf16[16,13,32,128]{3,2,1,0:T(8,128)(2,1)S(1)} collective-permute-done((bf16[16,13,32,128]{3,2,1,0:T(8,128)(2,1)S(1)}, bf16[16,13,32,128]{3,2,1,0:T(8,128)(2,1)S(1)}, u32[]{:S(2)}, u32[]{:S(2)}) %collective-permute-start.1) | collective-permute-done | bytes 1703968 | tf_op jit(solution)/shard_map/ppermute | solution.py:132
  102.0 0.4 add_convert_fusion
  102.5 45.7 %all_to_all.5 = bf16[16,13,32,128]{3,2,1,0:T(8,128)(2,1)S(1)} all-to-all(bf16[16,13,32,128]{3,2,1,0:T(8,128)(2,1)S(1)} %add_convert_fusion), channel_id=1, replica_groups=mesh['shard'=16,'rep'=2] {'shard'}, dimensions={0} | all-to-all | bytes 3407872 | tf_op jit(solution)/shard_map/all_to_all | solution.py:206
  148.1 0.2 convert_reduce_fusion
  148.4 0.1 collective-permute-start.2
  148.5 1.4 collective-permute-done.2
  149.9 0.2 multiply_reduce_fusion
  150.1 0.0 copy-done.8
  150.1 0.6 sqrt_add_fusion
  150.7 0.0 copy-done.7
  150.7 0.9 divide_subtract_fusion
  (11 shorter events, 0.1 us)
Async XLA Ops:
  7.2 69.6 %copy-start.3 = (bf16[128,1792]{1,0:T(8,128)(2,1)S(1)}, bf16[128,1792]{1,0:T(8,128)(2,1)}, u32[]{:S(2)}) copy-start(bf16[128,1792]{1,0:T(8,128)(2,1)} %cotangent.1) | copy-start | bytes 1376260
  7.2 65.8 %all-gather.3.cloned.1.call-start = ((), (), s32[]{:S(2)}) async-start(), calls=%async_computation.1 | async-start | bytes 1810432 | tf_op jit(solution)/shard_map/all_gather | solution.py:135
  72.9 3.8 %collective-permute-start = (bf16[16,13,32,128]{3,2,1,0:T(8,128)(2,1)}, bf16[16,13,32,128]{3,2,1,0:T(8,128)(2,1)S(1)}, u32[]{:S(2)}, u32[]{:S(2)}) collective-permute-start(bf16[16,13,32,128]{3,2,1,0:T(8,128)(2,1)} %bitcast.5), channel_id=1, source_target_pairs={{0,1},{1,0},{2,3},{3,2},{4,5},{5,4},{6,7},{7,6},{8,9},{9,8},{10,11... | collective-permute-start | bytes 5111816 | tf_op jit(solution)/shard_map/ppermute | solution.py:132
  76.7 1.5 copy-start
  78.2 1.5 copy-start.1
  79.7 1.5 copy-start.2
  81.2 0.9 copy-start.4
  82.2 0.8 copy-start.5
  83.0 0.7 copy-start.6
  98.4 3.6 %collective-permute-start.1 = (bf16[16,13,32,128]{3,2,1,0:T(8,128)(2,1)S(1)}, bf16[16,13,32,128]{3,2,1,0:T(8,128)(2,1)S(1)}, u32[]{:S(2)}, u32[]{:S(2)}) collective-permute-start(bf16[16,13,32,128]{3,2,1,0:T(8,128)(2,1)S(1)} %get-tuple-element.8), channel_id=1, source_target_pairs={{0,1},{1,0},{2,3},{3,2},{4,5},{5,4},{6,7},{7,6},{8,9},{9,8},{10,11... | collective-permute-start | bytes 5111816 | tf_op jit(solution)/shard_map/ppermute | solution.py:132
  148.1 2.0 %copy-start.8 = (f32[13,64]{1,0:T(8,128)S(1)}, f32[13,64]{1,0:T(8,128)}, u32[]{:S(2)}) copy-start(f32[13,64]{1,0:T(8,128)} %param.19) | copy-start | bytes 9988
  148.1 2.6 %copy-start.7 = (bf16[13,64,128]{2,1,0:T(8,128)(2,1)S(1)}, bf16[13,64,128]{2,1,0:T(8,128)(2,1)}, u32[]{:S(2)}) copy-start(bf16[13,64,128]{2,1,0:T(8,128)(2,1)} %param.18) | copy-start | bytes 638980
  148.4 1.5 collective-permute-start.2
Sparse Core Ops, SparseCore 0:
  11.3 61.5 all-gather.2
